TPU v7x, 32 devices: a whole 2x2x4 slice. The times are simulated.
32 devices in a mesh: dp: 8 (over z, x), tensor: 4 (over y, core).
Axes of the slice: x: 2, y: 2, z: 4, core: 2. Of those that a mesh axis runs over, the one named last changes fastest.
Arguments:
- tokens: bfloat16 [16384, 1024], P(('dp', 'tensor')), may hold values from -6 to 6
- cotangent: bfloat16 [16384, 1024], P(('dp', 'tensor')), may hold values from -6 to 6
- lengths: int32 [8, 16], P('dp'), may hold values from 1 to 256, 2048 in all within a row
- qkv_master: float32 [1024, 3, 1024], P('dp', None, 'tensor'), may hold values from -0.1875 to 0.1875
- qkv_first: float32 [1024, 3, 1024], P('dp', None, 'tensor'), may hold values from -0.00015258789 to 0.00015258789
- qkv_second: float32 [1024, 3, 1024], P('dp', None, 'tensor'), may hold values from 2.9798684e-11 to 4.7677895e-10
- out_master: float32 [1024, 1024], P(('tensor', 'dp')), may hold values from -1 to 1
- out_first: float32 [1024, 1024], P(('tensor', 'dp')), may hold values from -9.1552734e-05 to 9.1552734e-05
- out_second: float32 [1024, 1024], P(('tensor', 'dp')), may hold values from 5.959737e-12 to 9.535579e-11
- in_master: float32 [1024, 2, 4096], P('dp', None, 'tensor'), may hold values from -0.1875 to 0.1875
- in_first: float32 [1024, 2, 4096], P('dp', None, 'tensor'), may hold values from -0.00015258789 to 0.00015258789
- in_second: float32 [1024, 2, 4096], P('dp', None, 'tensor'), may hold values from 2.9798684e-11 to 4.7677895e-10
- down_master: float32 [4096, 1024], P(('tensor', 'dp')), may hold values from -0.09375 to 0.09375
- down_first: float32 [4096, 1024], P(('tensor', 'dp')), may hold values from -0.00015258789 to 0.00015258789
- down_second: float32 [4096, 1024], P(('tensor', 'dp')), may hold values from 2.9798684e-11 to 4.7677895e-10
- norm_gains: float32 [2, 1024], replicated, may hold values from 0.2 to 2.8
- gain_first: float32 [2, 1024], replicated, may hold values from -0.00061035156 to 0.00061035156
- gain_second: float32 [2, 1024], replicated, may hold values from 4.7677895e-10 to 7.628463e-09
Outputs:
- layer_out: bfloat16 [16384, 1024], P(('dp', 'tensor'))
- input_grad: float32 [16384, 1024], P(('dp', 'tensor'))
- qkv_grad: float32 [1024, 3, 1024], P('dp', None, 'tensor')
- qkv_new: float32 [1024, 3, 1024], P('dp', None, 'tensor')
- qkv_first_new: float32 [1024, 3, 1024], P('dp', None, 'tensor')
- qkv_second_new: float32 [1024, 3, 1024], P('dp', None, 'tensor')
- out_grad: float32 [1024, 1024], P(('tensor', 'dp'))
- out_new: float32 [1024, 1024], P(('tensor', 'dp'))
- out_first_new: float32 [1024, 1024], P(('tensor', 'dp'))
- out_second_new: float32 [1024, 1024], P(('tensor', 'dp'))
- in_grad: float32 [1024, 2, 4096], P('dp', None, 'tensor')
- in_new: float32 [1024, 2, 4096], P('dp', None, 'tensor')
- in_first_new: float32 [1024, 2, 4096], P('dp', None, 'tensor')
- in_second_new: float32 [1024, 2, 4096], P('dp', None, 'tensor')
- down_grad: float32 [4096, 1024], P(('tensor', 'dp'))
- down_new: float32 [4096, 1024], P(('tensor', 'dp'))
- down_first_new: float32 [4096, 1024], P(('tensor', 'dp'))
- down_second_new: float32 [4096, 1024], P(('tensor', 'dp'))
- gain_grad: float32 [2, 1024], replicated
- gain_new: float32 [2, 1024], replicated
- gain_first_new: float32 [2, 1024], replicated
- gain_second_new: float32 [2, 1024], replicated
- grad_norm: float32 [], replicated
Inputs may be any that keep to these rules, and one draw needn't show every extreme that they name: Each row's 16 window lengths are positive, add up to 2048, and the longest is 256.
All inputs are finite; a program needn't handle non-finite values.
Results may differ from a plain program's by a relative error of at most 0.024.
Values may be sent and summed in bfloat16 or wider, within the bound.
No kernel may reach another device: no remote copies, remote signals or barrier semaphores. Data moves between devices by JAX's collectives and lax.ppermute only.
A program may use at most 192 MiB of HBM per device.

v0:
```python
from functools import partial
import math
import jax
import jax.numpy as jnp
from jax import lax
from jax.sharding import PartitionSpec as P

D = 1024
HEADS = 16
HEAD_DIM = 64
FF = 4096
ROW = 2048
STEP = 5
eps_norm = 1e-05
beta_one = 0.9
beta_two = 0.999
learn_rate = 0.05
gain_rate = 0.6
weight_decay = 0.1
adam_eps = 1e-08
max_norm = 1.0


def layer_norm(values, gain):
    centre = values - jnp.mean(values, axis=-1, keepdims=True)
    spread = jnp.mean(centre * centre, axis=-1, keepdims=True)
    return centre * lax.rsqrt(spread + eps_norm) * gain


def row_layout(lengths):
    seg_ends = jnp.cumsum(lengths, axis=-1)
    places = jnp.arange(ROW, dtype=jnp.int32)
    passed = (places[:, None] >= seg_ends[..., None, :]).astype(jnp.int32)
    segment = jnp.sum(passed, axis=-1)
    offset = places - jnp.sum(passed * lengths[..., None, :], axis=-1)
    return (segment, offset)


def rotary_tables(offset):
    half_dim = HEAD_DIM // 2
    inverse = jnp.exp(
        jnp.arange(half_dim, dtype=jnp.float32) * (-2.0 * math.log(10000.0) / HEAD_DIM)
    )
    angles = offset.astype(jnp.float32)[..., None] * inverse
    return (jnp.cos(angles), jnp.sin(angles))


def rotate(values, cosine, sine):
    half_dim = values.shape[-1] // 2
    front_half = values[..., :half_dim]
    back_half = values[..., half_dim:]
    cos_wide = cosine[..., None, :]
    sin_wide = sine[..., None, :]
    return jnp.concatenate(
        [
            front_half * cos_wide - back_half * sin_wide,
            back_half * cos_wide + front_half * sin_wide,
        ],
        axis=-1,
    )


def swiglu(gate_up):
    half_cols = gate_up.shape[-1] // 2
    return jax.nn.silu(gate_up[:, :half_cols]) * gate_up[:, half_cols:]


def adam_update(weight, first_moment, second_moment, gradient, factor, use_decay, rate):
    clipped = gradient * factor
    first_new = beta_one * first_moment + (1.0 - beta_one) * clipped
    second_new = beta_two * second_moment + (1.0 - beta_two) * clipped * clipped
    first_hat = first_new / (1.0 - beta_one**STEP)
    second_hat = second_new / (1.0 - beta_two**STEP)
    direction = first_hat / (jnp.sqrt(second_hat) + adam_eps) + use_decay * weight_decay * weight
    return (clipped, weight - rate * direction, first_new, second_new)


def contract_rows(left, right):
    return lax.dot_general(
        left, right, (((0,), (0,)), ((), ())), preferred_element_type=jnp.float32
    )


def contract_cols(left, right):
    return lax.dot_general(
        left, right, (((1,), (1,)), ((), ())), preferred_element_type=jnp.float32
    )


def per_device(
    tokens,
    cotangent,
    lengths,
    qkv_master,
    qkv_first,
    qkv_second,
    out_master,
    out_first,
    out_second,
    in_master,
    in_first,
    in_second,
    down_master,
    down_first,
    down_second,
    norm_gains,
    gain_first,
    gain_second,
):
    heads_local = HEADS // lax.axis_size("tensor")
    width_local = heads_local * HEAD_DIM
    ffn_local = FF // lax.axis_size("tensor")
    row_count = lengths.shape[0]
    all_rows = row_count * ROW
    score_scale = HEAD_DIM ** (-0.5)
    block_rows = min(512, ROW)
    block_count = ROW // block_rows
    w_qkv, w_out, w_in, w_down = (
        lax.all_gather(qkv_master.astype(jnp.bfloat16), "dp", axis=0, tiled=True),
        lax.all_gather(out_master.astype(jnp.bfloat16), "dp", axis=0, tiled=True),
        lax.all_gather(in_master.astype(jnp.bfloat16), "dp", axis=0, tiled=True),
        lax.all_gather(down_master.astype(jnp.bfloat16), "dp", axis=0, tiled=True),
    )
    w_qkv = w_qkv.reshape(D, 3 * width_local)
    w_in = w_in.reshape(D, 2 * ffn_local)
    segment, offset = row_layout(lengths)
    cosine, sine = rotary_tables(offset)
    gain_one = norm_gains[0]
    gain_two = norm_gains[1]
    inputs = tokens.astype(jnp.float32)
    normed = layer_norm(inputs, gain_one)
    gathered_one = lax.all_gather(normed.astype(jnp.bfloat16), "tensor", axis=0, tiled=True)
    projected = jnp.dot(gathered_one, w_qkv, preferred_element_type=jnp.float32)
    projected = projected.reshape(row_count, ROW, 3, heads_local, HEAD_DIM)
    queries = rotate(projected[:, :, 0], cosine, sine).astype(jnp.bfloat16)
    keys = rotate(projected[:, :, 1], cosine, sine).astype(jnp.bfloat16)
    values = projected[:, :, 2].astype(jnp.bfloat16)

    def score_block(query_block, key_row, segment_block, segment_row):
        scores = (
            jnp.einsum("qhd,khd->hqk", query_block, key_row, preferred_element_type=jnp.float32)
            * score_scale
        )
        allowed = segment_block[:, None] == segment_row[None, :]
        return jnp.where(allowed[None], scores, -1e30)

    def forward_row(pieces):
        query_row, key_row, value_row, segment_row = pieces

        def forward_block(block_parts):
            query_block, segment_block = block_parts
            masked = score_block(query_block, key_row, segment_block, segment_row)
            row_max = jnp.max(masked, axis=-1, keepdims=True)
            log_total = (
                jnp.log(jnp.sum(jnp.exp(masked - row_max), axis=-1, keepdims=True)) + row_max
            )
            weights = jnp.exp(masked - log_total).astype(jnp.bfloat16)
            mixed_heads = jnp.einsum(
                "hqk,khd->qhd", weights, value_row, preferred_element_type=jnp.float32
            )
            return (mixed_heads.astype(jnp.bfloat16), log_total)

        return lax.map(
            forward_block,
            (
                query_row.reshape(block_count, block_rows, heads_local, HEAD_DIM),
                segment_row.reshape(block_count, block_rows),
            ),
        )

    mixed_heads, log_totals = lax.map(forward_row, (queries, keys, values, segment))
    attended = mixed_heads.reshape(all_rows, width_local)
    middle = inputs + lax.psum_scatter(
        jnp.dot(attended, w_out, preferred_element_type=jnp.float32),
        "tensor",
        scatter_dimension=0,
        tiled=True,
    )
    normed_two = layer_norm(middle, gain_two)
    gathered_two = lax.all_gather(normed_two.astype(jnp.bfloat16), "tensor", axis=0, tiled=True)
    gate_up = jnp.dot(gathered_two, w_in, preferred_element_type=jnp.float32)
    hidden = swiglu(gate_up).astype(jnp.bfloat16)
    output = middle + lax.psum_scatter(
        jnp.dot(hidden, w_down, preferred_element_type=jnp.float32).astype(jnp.bfloat16),
        "tensor",
        scatter_dimension=0,
        tiled=True,
    ).astype(jnp.float32)
    layer_out = output.astype(jnp.bfloat16)
    upstream = cotangent.astype(jnp.float32)
    gathered_down = lax.all_gather(cotangent, "tensor", axis=0, tiled=True)
    grad_down = contract_rows(hidden, gathered_down)
    hidden_grad = contract_cols(gathered_down, w_down)
    gate_up_grad = jax.vjp(swiglu, gate_up)[1](hidden_grad)[0].astype(jnp.bfloat16)
    grad_in = contract_rows(gathered_two, gate_up_grad)
    normed_two_grad = lax.psum_scatter(
        contract_cols(gate_up_grad, w_in).astype(jnp.bfloat16),
        "tensor",
        scatter_dimension=0,
        tiled=True,
    ).astype(jnp.float32)
    middle_back, gain_two_grad = jax.vjp(layer_norm, middle, gain_two)[1](normed_two_grad)
    middle_grad = upstream + middle_back
    gathered_mid = lax.all_gather(middle_grad.astype(jnp.bfloat16), "tensor", axis=0, tiled=True)
    grad_out = contract_rows(attended, gathered_mid)
    attended_grad = contract_cols(gathered_mid, w_out).astype(jnp.bfloat16)
    attended_grad = attended_grad.reshape(row_count, ROW, heads_local, HEAD_DIM)

    def backward_row(pieces):
        query_row, key_row, value_row, segment_row, total_row, grad_row = pieces

        def backward_block(running, block_parts):
            key_acc, value_acc = running
            query_block, segment_block, total_block, grad_block = block_parts
            masked = score_block(query_block, key_row, segment_block, segment_row)
            probs_block = jnp.exp(masked - total_block)
            probs_low = probs_block.astype(jnp.bfloat16)
            prob_grad = jnp.einsum(
                "qhd,khd->hqk", grad_block, value_row, preferred_element_type=jnp.float32
            )
            row_inner = jnp.sum(probs_block * prob_grad, axis=-1, keepdims=True)
            score_grad = (probs_block * (prob_grad - row_inner)).astype(jnp.bfloat16)
            query_grad = (
                jnp.einsum("hqk,khd->qhd", score_grad, key_row, preferred_element_type=jnp.float32)
                * score_scale
            )
            key_acc = (
                key_acc
                + jnp.einsum(
                    "hqk,qhd->khd", score_grad, query_block, preferred_element_type=jnp.float32
                )
                * score_scale
            )
            value_acc = value_acc + jnp.einsum(
                "hqk,qhd->khd", probs_low, grad_block, preferred_element_type=jnp.float32
            )
            return ((key_acc, value_acc), query_grad)

        zeros_acc = jnp.zeros((ROW, heads_local, HEAD_DIM), jnp.float32)
        block_inputs = (
            query_row.reshape(block_count, block_rows, heads_local, HEAD_DIM),
            segment_row.reshape(block_count, block_rows),
            total_row,
            grad_row.reshape(block_count, block_rows, heads_local, HEAD_DIM),
        )
        (key_grad, value_grad), query_grad = lax.scan(
            backward_block, (zeros_acc, zeros_acc), block_inputs
        )
        return (query_grad.reshape(ROW, heads_local, HEAD_DIM), key_grad, value_grad)

    query_grad, key_grad, value_grad = lax.map(
        backward_row, (queries, keys, values, segment, log_totals, attended_grad)
    )
    rotate_back = jax.vjp(partial(rotate, cosine=cosine, sine=sine), projected[:, :, 0])[1]
    query_raw = rotate_back(query_grad)[0]
    key_raw = rotate_back(key_grad)[0]
    qkv_grad_low = (
        jnp.stack([query_raw, key_raw, value_grad], axis=2)
        .reshape(all_rows, 3 * width_local)
        .astype(jnp.bfloat16)
    )
    grad_qkv = contract_rows(gathered_one, qkv_grad_low)
    normed_grad = lax.psum_scatter(
        contract_cols(qkv_grad_low, w_qkv).astype(jnp.bfloat16),
        "tensor",
        scatter_dimension=0,
        tiled=True,
    ).astype(jnp.float32)
    input_back, gain_one_grad = jax.vjp(layer_norm, inputs, gain_one)[1](normed_grad)
    input_grad = middle_grad + input_back
    reduced_qkv, reduced_out, reduced_in, reduced_down = (
        lax.psum_scatter(
            grad_qkv.reshape(D, 3, width_local).astype(jnp.bfloat16),
            "dp",
            scatter_dimension=0,
            tiled=True,
        ).astype(jnp.float32),
        lax.psum_scatter(
            grad_out.astype(jnp.bfloat16), "dp", scatter_dimension=0, tiled=True
        ).astype(jnp.float32),
        lax.psum_scatter(
            grad_in.reshape(D, 2, ffn_local).astype(jnp.bfloat16),
            "dp",
            scatter_dimension=0,
            tiled=True,
        ).astype(jnp.float32),
        lax.psum_scatter(
            grad_down.astype(jnp.bfloat16), "dp", scatter_dimension=0, tiled=True
        ).astype(jnp.float32),
    )
    local_squares = (
        jnp.sum(reduced_qkv * reduced_qkv)
        + jnp.sum(reduced_out * reduced_out)
        + jnp.sum(reduced_in * reduced_in)
        + jnp.sum(reduced_down * reduced_down)
    )
    gain_part = jnp.stack([gain_one_grad, gain_two_grad])
    gain_total, weight_squares = lax.psum((gain_part, local_squares), ("dp", "tensor"))
    grad_norm = jnp.sqrt(weight_squares + jnp.sum(gain_total * gain_total))
    factor = max_norm / jnp.maximum(grad_norm, max_norm)
    qkv_res = adam_update(qkv_master, qkv_first, qkv_second, reduced_qkv, factor, 1.0, learn_rate)
    out_res = adam_update(out_master, out_first, out_second, reduced_out, factor, 1.0, learn_rate)
    in_res = adam_update(in_master, in_first, in_second, reduced_in, factor, 1.0, learn_rate)
    down_res = adam_update(
        down_master, down_first, down_second, reduced_down, factor, 1.0, learn_rate
    )
    gain_res = adam_update(norm_gains, gain_first, gain_second, gain_total, factor, 0.0, gain_rate)
    return (
        layer_out,
        input_grad,
        qkv_res[0],
        qkv_res[1],
        qkv_res[2],
        qkv_res[3],
        out_res[0],
        out_res[1],
        out_res[2],
        out_res[3],
        in_res[0],
        in_res[1],
        in_res[2],
        in_res[3],
        down_res[0],
        down_res[1],
        down_res[2],
        down_res[3],
        gain_res[0],
        gain_res[1],
        gain_res[2],
        gain_res[3],
        grad_norm,
    )


def solution(mesh):
    placed = (
        P(("dp", "tensor"), None),
        P(("dp", "tensor"), None),
        P("dp", None),
        P("dp", None, "tensor"),
        P("dp", None, "tensor"),
        P("dp", None, "tensor"),
        P(("tensor", "dp"), None),
        P(("tensor", "dp"), None),
        P(("tensor", "dp"), None),
        P("dp", None, "tensor"),
        P("dp", None, "tensor"),
        P("dp", None, "tensor"),
        P(("tensor", "dp"), None),
        P(("tensor", "dp"), None),
        P(("tensor", "dp"), None),
        P(),
        P(),
        P(),
    )
    return jax.shard_map(
        per_device,
        mesh=mesh,
        in_specs=placed,
        out_specs=(
            P(("dp", "tensor"), None),
            P(("dp", "tensor"), None),
            P("dp", None, "tensor"),
            P("dp", None, "tensor"),
            P("dp", None, "tensor"),
            P("dp", None, "tensor"),
            P(("tensor", "dp"), None),
            P(("tensor", "dp"), None),
            P(("tensor", "dp"), None),
            P(("tensor", "dp"), None),
            P("dp", None, "tensor"),
            P("dp", None, "tensor"),
            P("dp", None, "tensor"),
            P("dp", None, "tensor"),
            P(("tensor", "dp"), None),
            P(("tensor", "dp"), None),
            P(("tensor", "dp"), None),
            P(("tensor", "dp"), None),
            P(),
            P(),
            P(),
            P(),
            P(),
        ),
        check_vma=False,
    )
```

profile of v0, /device:TPU:0, one launch (start us, length us, event | category | flops | bytes accessed | tf_op | source)
XLA Modules:
  0.0 1104.4 jit_solution(1875028781626215786)
XLA Ops:
  16.8 36.3 %all_gather.26 = bf16[256,1024]{1,0:T(8,128)(2,1)} all-gather(bf16[32,1024]{1,0:T(8,128)(2,1)S(1)} %convert_element_type.159), channel_id=1, replica_groups=mesh['dp'=8,'tensor'=4] {'dp'}, dimensions={0}, use_global_device_ids=true | all-gather | bytes 589824 | tf_op jit(solution)/shard_map/all_gather | solution.py:120
  61.6 35.9 %all-gather.8.cloned.1.call-done = bf16[2048,1024]{1,0:T(8,128)(2,1)} async-done(((bf16[512,1024]{1,0:T(8,128)(2,1)}), bf16[2048,1024]{1,0:T(8,128)(2,1)}) %all-gather.8.cloned.1.call-update) | async-done | bytes 4194320 | tf_op jit(solution)/shard_map/all_gather | solution.py:132
  110.1 57.2 %while.47 = (s32[]{:T(128)}, bf16[4,512,4,64]{1,3,2,0:T(8,128)(2,1)}, f32[4,4,512,1]{2,1,3,0:T(4,128)}, s32[4,512]{1,0:T(4,128)S(1)}, s32[2048]{0:T(1024)S(1)}, ...) while((s32[]{:T(128)}, ...), condition=%wide.region_8.9_spmd, body=%wide.region_5.8_spmd.sunk | while | flops 1121056768 | bytes 57227380 | solution.py:163
  178.4 69.5 %reduce-scatter.8.cloned.1.call-done = f32[512,1024]{1,0:T(8,128)} async-done(((f32[2048,1024]{1,0:T(8,128)}), f32[512,1024]{1,0:T(8,128)}) %reduce-scatter.8.cloned.1.call-update) | async-done | bytes 2097168 | tf_op jit(solution)/shard_map/reduce_scatter | solution.py:173
  254.4 69.7 %all-gather.14.cloned.1.call-done = bf16[1024,2,1024]{2,1,0:T(2,128)(2,1)} async-done(((bf16[128,2,1024]{2,1,0:T(2,128)(2,1)}), bf16[1024,2,1024]{2,1,0:T(2,128)(2,1)}) %all-gather.14.cloned.1.call-update) | async-done | bytes 4194320 | tf_op jit(solution)/shard_map/all_gather | solution.py:121
  329.7 29.2 %all-gather.12.cloned.1.call-done = bf16[2048,1024]{1,0:T(8,128)(2,1)} async-done(((bf16[512,1024]{1,0:T(8,128)(2,1)}), bf16[2048,1024]{1,0:T(8,128)(2,1)}) %all-gather.12.cloned.1.call-update) | async-done | bytes 4194320 | tf_op jit(solution)/shard_map/all_gather | solution.py:180
  358.9 15.1 %fusion.96 = f32[2048,2048]{1,0:T(8,128)} fusion(bf16[2048,1024]{1,0:T(8,128)(2,1)} %all-gather.12.cloned.1.call-done, bf16[1024,2048]{1,0:T(8,128)(2,1)} %bitcast.176), kind=kOutput, calls=%fused_computation.180 | convolution fusion | flops 8589934592 | bytes 25165824 | tf_op jit(solution)/shard_map/dot_general | solution.py:181
  374.0 37.0 %all-gather.16.cloned.1.call-done = bf16[1024,1024]{1,0:T(8,128)(2,1)} async-done(((bf16[128,1024]{1,0:T(8,128)(2,1)}), bf16[1024,1024]{1,0:T(8,128)(2,1)}) %all-gather.16.cloned.1.call-update) | async-done | bytes 2097168 | tf_op jit(solution)/shard_map/all_gather | solution.py:122
  411.0 34.6 %all-gather.18.cloned.1.call-done = bf16[2048,1024]{1,0:T(8,128)(2,1)} async-done(((bf16[512,1024]{1,0:T(8,128)(2,1)}), bf16[2048,1024]{1,0:T(8,128)(2,1)}) %all-gather.18.cloned.1.call-update) | async-done | bytes 4194320 | tf_op jit(solution)/shard_map/all_gather | solution.py:191
  445.6 17.2 %fusion.73 = (f32[2048,1024]{1,0:T(8,128)}, f32[2048,1024]{1,0:T(8,128)}, bf16[2048,1024]{1,0:T(8,128)(2,1)}) fusion(f32[2048,2048]{1,0:T(8,128)} %fusion.96, bf16[2048,1024]{1,0:T(8,128)(2,1)} %all-gather.18.cloned.1.call-done, bf16[1024,1024]{1,0:T(8,128)(2,1)} %all-gather.16.cloned.1.call-done), kind=kOutput, calls=%fused_computation.124 | convolution fusion | flops 4324327424 | bytes 44040192 | tf_op jit(solution)/shard_map/dot_general | solution.py:85
  462.8 15.0 %convolution_convert_fusion.1 = bf16[2048,1024]{1,0:T(8,128)(2,1)} fusion(bf16[1024,2048]{1,0:T(8,128)(2,1)} %bitcast.177, f32[2048,1024]{1,0:T(8,128)} %get-tuple-element.338, f32[2048,1024]{1,0:T(8,128)} %get-tuple-element.337), kind=kOutput, calls=%fused_computation.65 | convolution fusion | flops 8600420352 | bytes 25165824 | tf_op jit(solution)/shard_map/dot_general | solution.py:85
  478.4 9.6 convolution_convert_fusion.3
  488.0 34.6 %reduce-scatter.12.cloned.1.call-done = bf16[512,1024]{1,0:T(8,128)(2,1)} async-done(((bf16[2048,1024]{1,0:T(8,128)(2,1)}), bf16[512,1024]{1,0:T(8,128)(2,1)}) %reduce-scatter.12.cloned.1.call-update) | async-done | bytes 1048592 | tf_op jit(solution)/shard_map/reduce_scatter | solution.py:196
  525.3 44.4 %reduce-scatter.10.cloned.1.call-done = bf16[512,1024]{1,0:T(8,128)(2,1)} async-done(((bf16[2048,1024]{1,0:T(8,128)(2,1)}), bf16[512,1024]{1,0:T(8,128)(2,1)}) %reduce-scatter.10.cloned.1.call-update) | async-done | bytes 1048592 | tf_op jit(solution)/shard_map/reduce_scatter | solution.py:183
  575.8 17.0 %convolution_convert_fusion = bf16[1024,2048]{1,0:T(8,128)(2,1)} fusion(bf16[2048,1024]{1,0:T(8,128)(2,1)} %all-gather.12.cloned.1.call-done, f32[2048,1024]{1,0:T(8,128)} %get-tuple-element.338, f32[2048,1024]{1,0:T(8,128)} %get-tuple-element.337), kind=kOutput, calls=%fused_computation.64 | convolution fusion | flops 8600420352 | bytes 25165824 | tf_op jit(solution)/shard_map/dot_general | solution.py:79
  620.5 230.1 %while.48 = (s32[]{:T(128)}, f32[2048,4,64]{0,2,1:T(8,128)}, f32[2048,4,64]{0,2,1:T(8,128)}, f32[4,512,4,64]{1,0,3,2:T(4,128)}, bf16[4,512,4,64]{1,3,2,0:T(8,128...) while((s32[]{:T(128)}, f32[2048,4,64]{0,2,1:T(8,128)}, ...), condition=%wide.region_18.19_spmd.clone, body=%wide.region_16.18_spmd.clone.sunk | while | flops 2751068160 | bytes 183179600 | solution.py:246
  632.8 11.5 %multiply_reduce_fusion.4 = (f32[4,512]{1,0:T(4,128)}, f32[4,512,2048]{2,1,0:T(8,128)}) fusion(f32[4,512,2048]{2,1,0:T(8,128)S(1)} %fusion.154, f32[4,512]{1,0:T(4,128)S(1)} %dynamic-slice_bitcast_fusion.2, pred[512,2048]{1,0:T(8,128)(4,1)} %copy-done.1, bf16[2048,4,64]{0,2,1:T(8,128)(2,1)} %get-tuple-element.552, ...), kind=kOutput, calls=%fused_computation.20.clone.1 | convolution fusion | flops 557840384 | bytes 35930116 | tf_op jit(solution)/shard_map/while/body/eval_jaxpr/while/body/eval_jaxpr/qhd,khd->hqk/dot_general | solution.py:218
  644.4 11.2 %multiply_convert_fusion.4 = bf16[4,512,2048]{2,1,0:T(8,128)(2,1)} fusion(f32[4,512,2048]{2,1,0:T(8,128)} %get-tuple-element.487, f32[4,512,2048]{2,1,0:T(8,128)S(1)} %fusion.154, f32[4,512]{1,0:T(4,128)} %get-tuple-element.488, f32[4,512]{1,0:T(4,128)S(1)} %dynamic-slice_bitcast_fusion.2, pred[512,2048]{1,0:T(8,128)(4,1)} %copy-done.1), kind=kLoop, calls=%fused_computation.19.clone.1 | loop fusion | flops 25165824 | bytes 43008000 | tf_op jit(solution)/shard_map/while/body/eval_jaxpr/while/body/eval_jaxpr/convert_element_type | solution.py:222
  666.2 11.1 %dynamic_update_slice.33 = f32[4,512,4,64]{1,0,3,2:T(4,128)} dynamic-update-slice(f32[4,512,4,64]{1,0,3,2:T(4,128)} %get-tuple-element.532, f32[1,512,4,64]{1,0,3,2:T(1,128)S(1)} %copy.107, s32[]{:T(128)S(6)} %copy.125, s32[]{:T(128)} %constant.79.clone.1..sunk, s32[]{:T(128)} %constant.79.clone.1..sunk, s32[]{:T(128)} %constant.79.clone.1..sunk) | dynamic-update-slice | bytes 1048580 | tf_op jit(solution)/shard_map/while/body/eval_jaxpr/while/body/jit(dynamic_update_index_in_dim)/dynamic_update_slice | solution.py:246
  689.9 11.5 %multiply_reduce_fusion.4 = (f32[4,512]{1,0:T(4,128)}, f32[4,512,2048]{2,1,0:T(8,128)}) fusion(f32[4,512,2048]{2,1,0:T(8,128)S(1)} %fusion.154, f32[4,512]{1,0:T(4,128)S(1)} %dynamic-slice_bitcast_fusion.2, pred[512,2048]{1,0:T(8,128)(4,1)} %copy-done.1, bf16[2048,4,64]{0,2,1:T(8,128)(2,1)} %get-tuple-element.552, ...), kind=kOutput, calls=%fused_computation.20.clone.1 | convolution fusion | flops 557840384 | bytes 35930116 | tf_op jit(solution)/shard_map/while/body/eval_jaxpr/while/body/eval_jaxpr/qhd,khd->hqk/dot_general | solution.py:218
  701.4 11.0 %multiply_convert_fusion.4 = bf16[4,512,2048]{2,1,0:T(8,128)(2,1)} fusion(f32[4,512,2048]{2,1,0:T(8,128)} %get-tuple-element.487, f32[4,512,2048]{2,1,0:T(8,128)S(1)} %fusion.154, f32[4,512]{1,0:T(4,128)} %get-tuple-element.488, f32[4,512]{1,0:T(4,128)S(1)} %dynamic-slice_bitcast_fusion.2, pred[512,2048]{1,0:T(8,128)(4,1)} %copy-done.1), kind=kLoop, calls=%fused_computation.19.clone.1 | loop fusion | flops 25165824 | bytes 43008000 | tf_op jit(solution)/shard_map/while/body/eval_jaxpr/while/body/eval_jaxpr/convert_element_type | solution.py:222
  723.9 11.1 %dynamic_update_slice.33 = f32[4,512,4,64]{1,0,3,2:T(4,128)} dynamic-update-slice(f32[4,512,4,64]{1,0,3,2:T(4,128)} %get-tuple-element.532, f32[1,512,4,64]{1,0,3,2:T(1,128)S(1)} %copy.107, s32[]{:T(128)S(6)} %copy.125, s32[]{:T(128)} %constant.79.clone.1..sunk, s32[]{:T(128)} %constant.79.clone.1..sunk, s32[]{:T(128)} %constant.79.clone.1..sunk) | dynamic-update-slice | bytes 1048580 | tf_op jit(solution)/shard_map/while/body/eval_jaxpr/while/body/jit(dynamic_update_index_in_dim)/dynamic_update_slice | solution.py:246
  747.6 11.5 %multiply_reduce_fusion.4 = (f32[4,512]{1,0:T(4,128)}, f32[4,512,2048]{2,1,0:T(8,128)}) fusion(f32[4,512,2048]{2,1,0:T(8,128)S(1)} %fusion.154, f32[4,512]{1,0:T(4,128)S(1)} %dynamic-slice_bitcast_fusion.2, pred[512,2048]{1,0:T(8,128)(4,1)} %copy-done.1, bf16[2048,4,64]{0,2,1:T(8,128)(2,1)} %get-tuple-element.552, ...), kind=kOutput, calls=%fused_computation.20.clone.1 | convolution fusion | flops 557840384 | bytes 35930116 | tf_op jit(solution)/shard_map/while/body/eval_jaxpr/while/body/eval_jaxpr/qhd,khd->hqk/dot_general | solution.py:218
  759.2 11.0 multiply_convert_fusion.4
  781.6 11.1 %dynamic_update_slice.33 = f32[4,512,4,64]{1,0,3,2:T(4,128)} dynamic-update-slice(f32[4,512,4,64]{1,0,3,2:T(4,128)} %get-tuple-element.532, f32[1,512,4,64]{1,0,3,2:T(1,128)S(1)} %copy.107, s32[]{:T(128)S(6)} %copy.125, s32[]{:T(128)} %constant.79.clone.1..sunk, s32[]{:T(128)} %constant.79.clone.1..sunk, s32[]{:T(128)} %constant.79.clone.1..sunk) | dynamic-update-slice | bytes 1048580 | tf_op jit(solution)/shard_map/while/body/eval_jaxpr/while/body/jit(dynamic_update_index_in_dim)/dynamic_update_slice | solution.py:246
  805.3 11.5 %multiply_reduce_fusion.4 = (f32[4,512]{1,0:T(4,128)}, f32[4,512,2048]{2,1,0:T(8,128)}) fusion(f32[4,512,2048]{2,1,0:T(8,128)S(1)} %fusion.154, f32[4,512]{1,0:T(4,128)S(1)} %dynamic-slice_bitcast_fusion.2, pred[512,2048]{1,0:T(8,128)(4,1)} %copy-done.1, bf16[2048,4,64]{0,2,1:T(8,128)(2,1)} %get-tuple-element.552, ...), kind=kOutput, calls=%fused_computation.20.clone.1 | convolution fusion | flops 557840384 | bytes 35930116 | tf_op jit(solution)/shard_map/while/body/eval_jaxpr/while/body/eval_jaxpr/qhd,khd->hqk/dot_general | solution.py:218
  816.8 11.0 multiply_convert_fusion.4
  839.3 11.1 %dynamic_update_slice.33 = f32[4,512,4,64]{1,0,3,2:T(4,128)} dynamic-update-slice(f32[4,512,4,64]{1,0,3,2:T(4,128)} %get-tuple-element.532, f32[1,512,4,64]{1,0,3,2:T(1,128)S(1)} %copy.107, s32[]{:T(128)S(6)} %copy.125, s32[]{:T(128)} %constant.79.clone.1..sunk, s32[]{:T(128)} %constant.79.clone.1..sunk, s32[]{:T(128)} %constant.79.clone.1..sunk) | dynamic-update-slice | bytes 1048580 | tf_op jit(solution)/shard_map/while/body/eval_jaxpr/while/body/jit(dynamic_update_index_in_dim)/dynamic_update_slice | solution.py:246
  883.5 37.6 %reduce-scatter.18.cloned.1.call-done = bf16[32,1024]{1,0:T(8,128)(2,1)} async-done(((bf16[256,1024]{1,0:T(8,128)(2,1)}), bf16[32,1024]{1,0:T(8,128)(2,1)}) %reduce-scatter.18.cloned.1.call-update) | async-done | bytes 65552 | tf_op jit(solution)/shard_map/reduce_scatter | solution.py:278
  922.6 66.9 %reduce-scatter.16.cloned.1.call-done = bf16[128,3,256]{2,0,1:T(8,128)(2,1)} async-done(((bf16[1024,3,256]{2,0,1:T(8,128)(2,1)}), bf16[128,3,256]{2,0,1:T(8,128)(2,1)}) %reduce-scatter.16.cloned.1.call-update) | async-done | bytes 196624 | tf_op jit(solution)/shard_map/reduce_scatter | solution.py:272
  993.7 41.8 %reduce-scatter.14.cloned.1.call-done = bf16[512,1024]{1,0:T(8,128)(2,1)} async-done(((bf16[2048,1024]{1,0:T(8,128)(2,1)}), bf16[512,1024]{1,0:T(8,128)(2,1)}) %reduce-scatter.14.cloned.1.call-update) | async-done | bytes 1048592 | tf_op jit(solution)/shard_map/reduce_scatter | solution.py:263
  1039.7 39.7 %all-reduce.7 = (f32[]{:T(128)}, f32[2,1024]{1,0:T(2,128)S(1)}) all-reduce(f32[]{:T(128)S(6)} %add.210, f32[2,1024]{1,0:T(2,128)S(1)} %pad_maximum_fusion.1), channel_id=1, replica_groups=mesh['dp'=8,'tensor'=4] {'dp','tensor'}, use_global_device_ids=true, to_apply=%region_30.31 | all-reduce | flops 2049 | bytes 16392 | tf_op jit(solution)/shard_map/psum | solution.py:298
  (313 shorter events, 297.0 us)
Async XLA Ops:
  7.2 54.4 %all-gather.10.cloned.1.call-start = ((), (), s32[]{:S(2)}) async-start(), calls=%async_computation.8 | async-start | bytes 1769472 | tf_op jit(solution)/shard_map/all_gather | solution.py:119
  9.1 88.4 %all-gather.8.cloned.1.call-start = ((), (), s32[]{:S(2)}) async-start(), calls=%async_computation.7 | async-start | bytes 5242880 | tf_op jit(solution)/shard_map/all_gather | solution.py:132
  16.3 231.6 %reduce-scatter.8.cloned.1.call-start = ((), (), s32[]{:S(2)}) async-start(), calls=%async_computation.9 | async-start | bytes 10485760 | tf_op jit(solution)/shard_map/reduce_scatter | solution.py:173
  54.1 50.3 %copy-start.14 = (f32[2048,32]{0,1:T(8,128)}, f32[2048,32]{0,1:T(8,128)S(1)}, u32[]{:S(2)}) copy-start(f32[2048,32]{0,1:T(8,128)S(1)} %get-tuple-element.355) | copy-start | bytes 786436
  54.1 50.3 %copy-start.16 = (f32[2048,32]{0,1:T(8,128)}, f32[2048,32]{0,1:T(8,128)S(1)}, u32[]{:S(2)}) copy-start(f32[2048,32]{0,1:T(8,128)S(1)} %get-tuple-element.356) | copy-start | bytes 786436
  176.0 148.1 %all-gather.14.cloned.1.call-start = ((), (), s32[]{:S(2)}) async-start(), calls=%async_computation.11 | async-start | bytes 4718592 | tf_op jit(solution)/shard_map/all_gather | solution.py:121
  178.4 180.5 %all-gather.12.cloned.1.call-start = ((), (), s32[]{:S(2)}) async-start(), calls=%async_computation.10 | async-start | bytes 5242880 | tf_op jit(solution)/shard_map/all_gather | solution.py:180
  251.7 159.3 %all-gather.16.cloned.1.call-start = ((), (), s32[]{:S(2)}) async-start(), calls=%async_computation.12 | async-start | bytes 2359296 | tf_op jit(solution)/shard_map/all_gather | solution.py:122
  253.6 192.1 %all-gather.18.cloned.1.call-start = ((), (), s32[]{:S(2)}) async-start(), calls=%async_computation.14 | async-start | bytes 5242880 | tf_op jit(solution)/shard_map/all_gather | solution.py:191
  254.3 268.3 %reduce-scatter.12.cloned.1.call-start = ((), (), s32[]{:S(2)}) async-start(), calls=%async_computation.15 | async-start | bytes 5242880 | tf_op jit(solution)/shard_map/reduce_scatter | solution.py:196
  477.9 91.8 %reduce-scatter.10.cloned.1.call-start = ((), (), s32[]{:S(2)}) async-start(), calls=%async_computation.13 | async-start | bytes 5242880 | tf_op jit(solution)/shard_map/reduce_scatter | solution.py:183
  488.0 122.4 %all-gather.20.cloned.1.call-start = ((), (), s32[]{:S(2)}) async-start(), calls=%async_computation.16 | async-start | bytes 5242880 | tf_op jit(solution)/shard_map/all_gather | solution.py:204
  573.1 19.7 %copy-start.45 = (f32[512]{0:T(512)}, f32[512]{0:T(512)S(1)}, u32[]{:S(2)}) copy-start(f32[512]{0:T(512)S(1)} %negate_multiply_fusion.1) | copy-start | bytes 6148
  575.7 303.3 %all-reduce.10.cloned.1.call-start = ((), (), s32[]{:S(2)}) async-start(), calls=%async_computation.21 | async-start | bytes 8388608
  600.7 281.1 %reduce-scatter.20.cloned.1.call-start = ((), (), s32[]{:S(2)}) async-start(), calls=%async_computation.20 | async-start | bytes 2359296 | tf_op jit(solution)/shard_map/reduce_scatter | solution.py:287
  610.3 310.8 %reduce-scatter.18.cloned.1.call-start = ((), (), s32[]{:S(2)}) async-start(), calls=%async_computation.19 | async-start | bytes 589824 | tf_op jit(solution)/shard_map/reduce_scatter | solution.py:278
  718.7 16.4 %copy-start.22 = (s32[2048]{0:T(1024)S(1)}, s32[2048]{0:T(1024)}, u32[]{:S(2)}) copy-start(s32[2048]{0:T(1024)} %copy-done.21) | copy-start | bytes 24580 | tf_op jit(solution)/shard_map/while/body/eval_jaxpr/while
  718.7 16.4 %copy-start.39 = (s32[4,512]{1,0:T(4,128)S(1)}, s32[4,512]{1,0:T(4,128)}, u32[]{:S(2)}) copy-start(s32[4,512]{1,0:T(4,128)} %copy-done.38) | copy-start | bytes 24580 | tf_op jit(solution)/shard_map/while/body/eval_jaxpr/while
  776.4 16.3 %copy-start.22 = (s32[2048]{0:T(1024)S(1)}, s32[2048]{0:T(1024)}, u32[]{:S(2)}) copy-start(s32[2048]{0:T(1024)} %copy-done.21) | copy-start | bytes 24580 | tf_op jit(solution)/shard_map/while/body/eval_jaxpr/while
  858.7 130.7 %reduce-scatter.16.cloned.1.call-start = ((), (), s32[]{:S(2)}) async-start(), calls=%async_computation.18 | async-start | bytes 1769472 | tf_op jit(solution)/shard_map/reduce_scatter | solution.py:272
  870.1 165.4 %reduce-scatter.14.cloned.1.call-start = ((), (), s32[]{:S(2)}) async-start(), calls=%async_computation.17 | async-start | bytes 5242880 | tf_op jit(solution)/shard_map/reduce_scatter | solution.py:263
  877.2 158.3 %copy-start.3 = (bf16[512,1024]{1,0:T(8,128)(2,1)S(1)}, bf16[512,1024]{1,0:T(8,128)(2,1)}, u32[]{:S(2)}) copy-start(bf16[512,1024]{1,0:T(8,128)(2,1)} %param.22) | copy-start | bytes 3145732
  877.2 158.3 %copy-start.37 = (f32[1,1024]{1,0:T(1,128)S(1)}, f32[1,1024]{1,0:T(1,128)}, u32[]{:S(2)}) copy-start(f32[1,1024]{1,0:T(1,128)} %copy-done.36) | copy-start | bytes 12292
  877.2 158.3 %copy-start.41 = (f32[512]{0:T(512)S(1)}, f32[512]{0:T(512)}, u32[]{:S(2)}) copy-start(f32[512]{0:T(512)} %copy-done.40) | copy-start | bytes 6148
  877.2 160.1 %copy-start.48 = (f32[512]{0:T(512)S(1)}, f32[512]{0:T(512)}, u32[]{:S(2)}) copy-start(f32[512]{0:T(512)} %copy-done.47) | copy-start | bytes 6148
  877.2 160.1 %copy-start.44 = (f32[512]{0:T(512)S(1)}, f32[512]{0:T(512)}, u32[]{:S(2)}) copy-start(f32[512]{0:T(512)} %copy-done.43) | copy-start | bytes 6148
  877.2 162.5 %copy-start.49 = (f32[1024]{0:T(1024)S(1)}, f32[1024]{0:T(1024)}, u32[]{:S(2)}) copy-start(f32[1024]{0:T(1024)} %get-tuple-element.261) | copy-start | bytes 12292
  877.2 204.3 %copy-start.42 = (f32[2,1024]{1,0:T(2,128)S(1)}, f32[2,1024]{1,0:T(2,128)}, u32[]{:S(2)}) copy-start(f32[2,1024]{1,0:T(2,128)} %param.37) | copy-start | bytes 24580
  877.2 204.3 %copy-start.50 = (f32[2,1024]{1,0:T(2,128)S(1)}, f32[2,1024]{1,0:T(2,128)}, u32[]{:S(2)}) copy-start(f32[2,1024]{1,0:T(2,128)} %param.38) | copy-start | bytes 24580
  877.2 204.3 %copy-start.51 = (f32[2,1024]{1,0:T(2,128)S(1)}, f32[2,1024]{1,0:T(2,128)}, u32[]{:S(2)}) copy-start(f32[2,1024]{1,0:T(2,128)} %param.39) | copy-start | bytes 24580
  877.3 204.9 %copy-start.7 = (f32[512,1024]{1,0:T(8,128)S(1)}, f32[512,1024]{1,0:T(8,128)}, u32[]{:S(2)}) copy-start(f32[512,1024]{1,0:T(8,128)} %copy-done.6) | copy-start | bytes 6291460
  877.3 204.9 %copy-start.46 = (f32[512]{0:T(512)S(1)}, f32[512]{0:T(512)}, u32[]{:S(2)}) copy-start(f32[512]{0:T(512)} %copy-done.45) | copy-start | bytes 6148
  (57 other events, 324.8 us)
Sparse Core Ops, SparseCore 0:
  10.7 50.9 all-gather.9
  63.8 33.7 all-gather.7
  176.1 71.7 reduce-scatter.7
  250.6 73.3 all-gather.13
  326.1 32.7 all-gather.11
  361.7 49.2 all-gather.15
  412.6 32.9 all-gather.17
  478.0 44.5 reduce-scatter.11
  525.1 44.5 reduce-scatter.9
  575.9 34.4 all-gather.19
  614.5 156.3 all-reduce.9
  774.7 66.9 reduce-scatter.19
  858.9 62.1 reduce-scatter.17
  925.0 64.4 reduce-scatter.15
  992.0 43.4 reduce-scatter.13
where the time goes:
time: 1110 us; the launch traced here: 1100 us
  waiting for transfers between devices  510 us (46%)
  matrix products  283 us (25%)
  other arithmetic  125 us (11%)
  local copies, waits for them, and re-layouts  88.5 us (8%)
  blocking collectives  76 us (7%)
  between operations  20.7 us (2%)
    all_gather x1, waiting for transfers between devices, per_device(): lax.all_gather(in_master.astype(jnp.bfloat16), 'dp', axis=0, tiled=True)  69.7 us
    reduce_scatter x1, waiting for transfers between devices, per_device(): lax.psum_scatter(jnp.dot(attended, w_out, preferred_element_type=jnp.floa...  69.5 us
    reduce_scatter x1, waiting for transfers between devices, per_device(): lax.psum_scatter(grad_qkv.reshape(D, 3, width_local).astype(jnp.bfloat16)...  66.9 us
    dynamic_update_slice x8, local copies, waits for them, and re-layouts, backward_row(): lax.scan(backward_block, (zeros_acc, zeros_acc), block_inputs)  46.6 us
    dot_general x4, matrix products, backward_block(): jnp.einsum('qhd,khd->hqk', grad_block, value_row, preferred_element_type=...  46.1 us
    reduce_scatter x1, waiting for transfers between devices, per_device(): lax.psum_scatter(jnp.dot(hidden, w_down, preferred_element_type=jnp.float...  44.4 us
    convert_element_type x4, other arithmetic, backward_block(): score_grad = (probs_block * (prob_grad - row_inner)).astype(jnp.bfloat16)  44.2 us
    dot_general x4, matrix products, contract_cols(): lax.dot_general(left, right, (((1,), (1,)), ((), ())), preferred_element_...  43.7 us
  transfers between devices with their start and end apart: 15, of which 13 were waited for; matrix products, arithmetic and copies ran while one was open for 32% of the time, Pallas kernels for 0%

commit v1 on v0

--- a/solution.py
+++ b/solution.py
@@ -19,6 +19,34 @@
 weight_decay = 0.1
 adam_eps = 1e-08
 max_norm = 1.0
+
+
+def _watch_axis_part(local_array, array_axis):
+    pages = []
+    x_next, carry, w1 = (lax.axis_size("dp"), lax.axis_index("dp"), local_array.shape[array_axis])
+    for w in range(x_next):
+        pages.append((w, (w + 1) % x_next))
+    views = []
+    for w in range(x_next):
+        views.append((w, (w - 1) % x_next))
+    response = jnp.zeros(
+        (*local_array.shape[:array_axis], x_next * w1, *local_array.shape[array_axis + 1 :]),
+        local_array.dtype,
+    )
+    y_new = wide_out = local_array
+    response = lax.dynamic_update_slice_in_dim(response, local_array, carry * w1, axis=array_axis)
+    y2 = x_next // 2
+    for u in range(1, y2 + 1):
+        y_new = lax.ppermute(y_new, "dp", perm=pages)
+        response = lax.dynamic_update_slice_in_dim(
+            response, y_new, (carry - u) % x_next * w1, axis=array_axis
+        )
+        if u < x_next - y2:
+            wide_out = lax.ppermute(wide_out, "dp", perm=views)
+            response = lax.dynamic_update_slice_in_dim(
+                response, wide_out, (carry + u) % x_next * w1, axis=array_axis
+            )
+    return response
 
 
 def layer_norm(values, gain):
@@ -118,7 +146,7 @@
     w_qkv, w_out, w_in, w_down = (
         lax.all_gather(qkv_master.astype(jnp.bfloat16), "dp", axis=0, tiled=True),
         lax.all_gather(out_master.astype(jnp.bfloat16), "dp", axis=0, tiled=True),
-        lax.all_gather(in_master.astype(jnp.bfloat16), "dp", axis=0, tiled=True),
+        _watch_axis_part(in_master.astype(jnp.bfloat16), 0),
         lax.all_gather(down_master.astype(jnp.bfloat16), "dp", axis=0, tiled=True),
     )
     w_qkv = w_qkv.reshape(D, 3 * width_local)

time: 1110 us -> 1060 us (0.955)
  waiting for transfers between devices: 510 us -> 424 us
  starting transfers between devices: 1.2 us -> 19.5 us
  local copies, waits for them, and re-layouts: 88.5 us -> 105 us
    ppermute x0 -> x7, waiting for transfers between devices: none -> 74.5 us  [the longest x4 74.5 us: _watch_axis_part(): y_new = lax.ppermute(y_new, 'dp', perm=pages)]
    all_gather x1 -> x0, waiting for transfers between devices: 69.7 us -> none  [per_device(): lax.all_gather(in_master.astype(jnp.bfloat16), 'dp', axis=0, tiled=True)]
    all_gather x1, waiting for transfers between devices: 37 us -> 0.01 us  [per_device(): lax.all_gather(down_master.astype(jnp.bfloat16), 'dp', axis=0, tiled=True)]
    all_gather x1, waiting for transfers between devices: 29.2 us -> 0.01 us  [per_device(): lax.all_gather(normed_two.astype(jnp.bfloat16), 'tensor', axis=0, tiled=T...]
    all_gather x1, waiting for transfers between devices: 34.6 us -> 8.26 us  [per_device(): gathered_down = lax.all_gather(cotangent, 'tensor', axis=0, tiled=True)]
    ppermute x0 -> x7, starting transfers between devices: none -> 18.6 us  [the longest x3 9.59 us: _watch_axis_part(): wide_out = lax.ppermute(wide_out, 'dp', perm=views)]
    dynamic_update_slice x0 -> x7, local copies, waits for them, and re-layouts: none -> 13.3 us  [the longest x4 7.78 us: _watch_axis_part(): lax.dynamic_update_slice_in_dim(response, y_new, (carry - u) % x_next * w...]
  transfers between devices with their start and end apart: 15 -> 21, of which waited for: 13 -> 13; matrix products, arithmetic and copies ran while one was open for 32% -> 35% of each run, Pallas kernels for 0% -> 0%
where the time goes in v1:
time: 1060 us
  waiting for transfers between devices  424 us (40%)
  matrix products  283 us (27%)
  other arithmetic  125 us (12%)
  local copies, waits for them, and re-layouts  105 us (10%)
  blocking collectives  76 us (7%)
  between operations  20.7 us (2%)
  starting transfers between devices  19.5 us (2%)
    ppermute x4, waiting for transfers between devices, _watch_axis_part(): y_new = lax.ppermute(y_new, 'dp', perm=pages)  74.5 us
    reduce_scatter x1, waiting for transfers between devices, per_device(): lax.psum_scatter(jnp.dot(attended, w_out, preferred_element_type=jnp.floa...  71.6 us
    reduce_scatter x1, waiting for transfers between devices, per_device(): lax.psum_scatter(grad_qkv.reshape(D, 3, width_local).astype(jnp.bfloat16)...  67 us
    dynamic_update_slice x8, local copies, waits for them, and re-layouts, backward_row(): lax.scan(backward_block, (zeros_acc, zeros_acc), block_inputs)  46.6 us
    dot_general x4, matrix products, backward_block(): jnp.einsum('qhd,khd->hqk', grad_block, value_row, preferred_element_type=...  46.2 us
    reduce_scatter x1, waiting for transfers between devices, per_device(): lax.psum_scatter(jnp.dot(hidden, w_down, preferred_element_type=jnp.float...  44.4 us
    convert_element_type x4, other arithmetic, backward_block(): score_grad = (probs_block * (prob_grad - row_inner)).astype(jnp.bfloat16)  44.2 us
    dot_general x4, matrix products, contract_cols(): lax.dot_general(left, right, (((1,), (1,)), ((), ())), preferred_element_...  43.8 us
  transfers between devices with their start and end apart: 21, of which 13 were waited for; matrix products, arithmetic and copies ran while one was open for 35% of the time, Pallas kernels for 0%

profile of v1, /device:TPU:0, one launch (start us, length us, event | category | flops | bytes accessed | tf_op | source)
XLA Modules:
  0.0 1055.0 jit_solution(15009828789300184077)
XLA Ops:
  16.8 36.3 %all_gather.23 = bf16[256,1024]{1,0:T(8,128)(2,1)} all-gather(bf16[32,1024]{1,0:T(8,128)(2,1)S(1)} %convert_element_type.159), channel_id=1, replica_groups=mesh['dp'=8,'tensor'=4] {'dp'}, dimensions={0}, use_global_device_ids=true | all-gather | bytes 589824 | tf_op jit(solution)/shard_map/all_gather | solution.py:148
  61.6 35.9 %all-gather.7.cloned.1.call-done = bf16[2048,1024]{1,0:T(8,128)(2,1)} async-done(((bf16[512,1024]{1,0:T(8,128)(2,1)}), bf16[2048,1024]{1,0:T(8,128)(2,1)}) %all-gather.7.cloned.1.call-update) | async-done | bytes 4194320 | tf_op jit(solution)/shard_map/all_gather | solution.py:160
  110.1 57.2 %while.47 = (s32[]{:T(128)}, bf16[4,512,4,64]{1,3,2,0:T(8,128)(2,1)}, f32[4,4,512,1]{2,1,3,0:T(4,128)}, s32[4,512]{1,0:T(4,128)S(1)}, s32[2048]{0:T(1024)S(1)}, ...) while((s32[]{:T(128)}, ...), condition=%wide.region_8.9_spmd, body=%wide.region_5.8_spmd.sunk | while | flops 1121056768 | bytes 57227380 | solution.py:191
  176.2 71.6 %reduce-scatter.8.cloned.1.call-done = f32[512,1024]{1,0:T(8,128)} async-done(((f32[2048,1024]{1,0:T(8,128)}), f32[512,1024]{1,0:T(8,128)}) %reduce-scatter.8.cloned.1.call-update) | async-done | bytes 2097168 | tf_op jit(solution)/shard_map/reduce_scatter | solution.py:201
  264.4 19.2 %collective-permute-done = bf16[128,2,1024]{2,1,0:T(2,128)(2,1)S(1)} collective-permute-done((bf16[128,2,1024]{2,1,0:T(2,128)(2,1)S(1)}, bf16[128,2,1024]{2,1,0:T(2,128)(2,1)S(1)}, u32[]{:S(2)}, u32[]{:S(2)}) %collective-permute-start) | collective-permute-done | bytes 524320 | tf_op jit(solution)/shard_map/ppermute | solution.py:40
  289.6 20.9 %collective-permute-done.2 = bf16[128,2,1024]{2,1,0:T(2,128)(2,1)} collective-permute-done((bf16[128,2,1024]{2,1,0:T(2,128)(2,1)S(1)}, bf16[128,2,1024]{2,1,0:T(2,128)(2,1)}, u32[]{:S(2)}, u32[]{:S(2)}) %collective-permute-start.2) | collective-permute-done | bytes 524320 | tf_op jit(solution)/shard_map/ppermute | solution.py:40
  318.1 27.8 %collective-permute-done.4 = bf16[128,2,1024]{2,1,0:T(2,128)(2,1)} collective-permute-done((bf16[128,2,1024]{2,1,0:T(2,128)(2,1)}, bf16[128,2,1024]{2,1,0:T(2,128)(2,1)}, u32[]{:S(2)}, u32[]{:S(2)}) %collective-permute-start.4) | collective-permute-done | bytes 524320 | tf_op jit(solution)/shard_map/ppermute | solution.py:40
  372.1 15.5 %fusion.96 = f32[2048,2048]{1,0:T(8,128)} fusion(bf16[2048,1024]{1,0:T(8,128)(2,1)} %all-gather.11.cloned.1.call-done, bf16[1024,2048]{1,0:T(8,128)(2,1)} %bitcast.175), kind=kOutput, calls=%fused_computation.188 | convolution fusion | flops 8589934592 | bytes 25165824 | tf_op jit(solution)/shard_map/dot_general | solution.py:209
  395.9 17.2 %fusion.73 = (f32[2048,1024]{1,0:T(8,128)}, f32[2048,1024]{1,0:T(8,128)}, bf16[2048,1024]{1,0:T(8,128)(2,1)}) fusion(f32[2048,2048]{1,0:T(8,128)} %fusion.96, bf16[2048,1024]{1,0:T(8,128)(2,1)} %all-gather.15.cloned.1.call-done, bf16[1024,1024]{1,0:T(8,128)(2,1)} %all-gather.13.cloned.1.call-done), kind=kOutput, calls=%fused_computation.124 | convolution fusion | flops 4324327424 | bytes 44040192 | tf_op jit(solution)/shard_map/dot_general | solution.py:113
  413.1 15.1 %convolution_convert_fusion.1 = bf16[2048,1024]{1,0:T(8,128)(2,1)} fusion(bf16[1024,2048]{1,0:T(8,128)(2,1)} %bitcast.176, f32[2048,1024]{1,0:T(8,128)} %get-tuple-element.340, f32[2048,1024]{1,0:T(8,128)} %get-tuple-element.339), kind=kOutput, calls=%fused_computation.65 | convolution fusion | flops 8600420352 | bytes 25165824 | tf_op jit(solution)/shard_map/dot_general | solution.py:113
  428.5 9.6 convolution_convert_fusion.3
  438.2 34.7 %reduce-scatter.12.cloned.1.call-done = bf16[512,1024]{1,0:T(8,128)(2,1)} async-done(((bf16[2048,1024]{1,0:T(8,128)(2,1)}), bf16[512,1024]{1,0:T(8,128)(2,1)}) %reduce-scatter.12.cloned.1.call-update) | async-done | bytes 1048592 | tf_op jit(solution)/shard_map/reduce_scatter | solution.py:224
  475.6 44.4 %reduce-scatter.10.cloned.1.call-done = bf16[512,1024]{1,0:T(8,128)(2,1)} async-done(((bf16[2048,1024]{1,0:T(8,128)(2,1)}), bf16[512,1024]{1,0:T(8,128)(2,1)}) %reduce-scatter.10.cloned.1.call-update) | async-done | bytes 1048592 | tf_op jit(solution)/shard_map/reduce_scatter | solution.py:211
  526.1 17.1 %convolution_convert_fusion = bf16[1024,2048]{1,0:T(8,128)(2,1)} fusion(bf16[2048,1024]{1,0:T(8,128)(2,1)} %all-gather.11.cloned.1.call-done, f32[2048,1024]{1,0:T(8,128)} %get-tuple-element.340, f32[2048,1024]{1,0:T(8,128)} %get-tuple-element.339), kind=kOutput, calls=%fused_computation.64 | convolution fusion | flops 8600420352 | bytes 25165824 | tf_op jit(solution)/shard_map/dot_general | solution.py:107
  551.1 9.5 convolution_convert_fusion.5
  570.8 230.6 %while.48 = (s32[]{:T(128)}, f32[2048,4,64]{0,2,1:T(8,128)}, f32[2048,4,64]{0,2,1:T(8,128)}, f32[4,512,4,64]{1,0,3,2:T(4,128)}, bf16[4,512,4,64]{1,3,2,0:T(8,128...) while((s32[]{:T(128)}, f32[2048,4,64]{0,2,1:T(8,128)}, ...), condition=%wide.region_18.19_spmd.clone, body=%wide.region_16.18_spmd.clone.sunk | while | flops 2751068160 | bytes 183179600 | solution.py:274
  583.4 11.5 %multiply_reduce_fusion.4 = (f32[4,512]{1,0:T(4,128)}, f32[4,512,2048]{2,1,0:T(8,128)}) fusion(f32[4,512,2048]{2,1,0:T(8,128)S(1)} %fusion.154, f32[4,512]{1,0:T(4,128)S(1)} %dynamic-slice_bitcast_fusion.2, pred[512,2048]{1,0:T(8,128)(4,1)} %copy-done.1, bf16[2048,4,64]{0,2,1:T(8,128)(2,1)} %get-tuple-element.554, ...), kind=kOutput, calls=%fused_computation.20.clone.1 | convolution fusion | flops 557840384 | bytes 35930116 | tf_op jit(solution)/shard_map/while/body/eval_jaxpr/while/body/eval_jaxpr/qhd,khd->hqk/dot_general | solution.py:246
  594.9 11.1 %multiply_convert_fusion.4 = bf16[4,512,2048]{2,1,0:T(8,128)(2,1)} fusion(f32[4,512,2048]{2,1,0:T(8,128)} %get-tuple-element.489, f32[4,512,2048]{2,1,0:T(8,128)S(1)} %fusion.154, f32[4,512]{1,0:T(4,128)} %get-tuple-element.490, f32[4,512]{1,0:T(4,128)S(1)} %dynamic-slice_bitcast_fusion.2, pred[512,2048]{1,0:T(8,128)(4,1)} %copy-done.1), kind=kLoop, calls=%fused_computation.19.clone.1 | loop fusion | flops 25165824 | bytes 43008000 | tf_op jit(solution)/shard_map/while/body/eval_jaxpr/while/body/eval_jaxpr/convert_element_type | solution.py:250
  616.8 11.1 %dynamic_update_slice.73 = f32[4,512,4,64]{1,0,3,2:T(4,128)} dynamic-update-slice(f32[4,512,4,64]{1,0,3,2:T(4,128)} %get-tuple-element.534, f32[1,512,4,64]{1,0,3,2:T(1,128)S(1)} %copy.107, s32[]{:T(128)S(6)} %copy.133, s32[]{:T(128)} %constant.205.clone.1..sunk, s32[]{:T(128)} %constant.205.clone.1..sunk, s32[]{:T(128)} %constant.205.clone.1..sunk) | dynamic-update-slice | bytes 1048580 | tf_op jit(solution)/shard_map/while/body/eval_jaxpr/while/body/jit(dynamic_update_index_in_dim)/dynamic_update_slice | solution.py:274
  640.5 11.6 %multiply_reduce_fusion.4 = (f32[4,512]{1,0:T(4,128)}, f32[4,512,2048]{2,1,0:T(8,128)}) fusion(f32[4,512,2048]{2,1,0:T(8,128)S(1)} %fusion.154, f32[4,512]{1,0:T(4,128)S(1)} %dynamic-slice_bitcast_fusion.2, pred[512,2048]{1,0:T(8,128)(4,1)} %copy-done.1, bf16[2048,4,64]{0,2,1:T(8,128)(2,1)} %get-tuple-element.554, ...), kind=kOutput, calls=%fused_computation.20.clone.1 | convolution fusion | flops 557840384 | bytes 35930116 | tf_op jit(solution)/shard_map/while/body/eval_jaxpr/while/body/eval_jaxpr/qhd,khd->hqk/dot_general | solution.py:246
  652.0 11.1 %multiply_convert_fusion.4 = bf16[4,512,2048]{2,1,0:T(8,128)(2,1)} fusion(f32[4,512,2048]{2,1,0:T(8,128)} %get-tuple-element.489, f32[4,512,2048]{2,1,0:T(8,128)S(1)} %fusion.154, f32[4,512]{1,0:T(4,128)} %get-tuple-element.490, f32[4,512]{1,0:T(4,128)S(1)} %dynamic-slice_bitcast_fusion.2, pred[512,2048]{1,0:T(8,128)(4,1)} %copy-done.1), kind=kLoop, calls=%fused_computation.19.clone.1 | loop fusion | flops 25165824 | bytes 43008000 | tf_op jit(solution)/shard_map/while/body/eval_jaxpr/while/body/eval_jaxpr/convert_element_type | solution.py:250
  674.7 11.1 %dynamic_update_slice.73 = f32[4,512,4,64]{1,0,3,2:T(4,128)} dynamic-update-slice(f32[4,512,4,64]{1,0,3,2:T(4,128)} %get-tuple-element.534, f32[1,512,4,64]{1,0,3,2:T(1,128)S(1)} %copy.107, s32[]{:T(128)S(6)} %copy.133, s32[]{:T(128)} %constant.205.clone.1..sunk, s32[]{:T(128)} %constant.205.clone.1..sunk, s32[]{:T(128)} %constant.205.clone.1..sunk) | dynamic-update-slice | bytes 1048580 | tf_op jit(solution)/shard_map/while/body/eval_jaxpr/while/body/jit(dynamic_update_index_in_dim)/dynamic_update_slice | solution.py:274
  698.4 11.6 %multiply_reduce_fusion.4 = (f32[4,512]{1,0:T(4,128)}, f32[4,512,2048]{2,1,0:T(8,128)}) fusion(f32[4,512,2048]{2,1,0:T(8,128)S(1)} %fusion.154, f32[4,512]{1,0:T(4,128)S(1)} %dynamic-slice_bitcast_fusion.2, pred[512,2048]{1,0:T(8,128)(4,1)} %copy-done.1, bf16[2048,4,64]{0,2,1:T(8,128)(2,1)} %get-tuple-element.554, ...), kind=kOutput, calls=%fused_computation.20.clone.1 | convolution fusion | flops 557840384 | bytes 35930116 | tf_op jit(solution)/shard_map/while/body/eval_jaxpr/while/body/eval_jaxpr/qhd,khd->hqk/dot_general | solution.py:246
  710.0 11.0 %multiply_convert_fusion.4 = bf16[4,512,2048]{2,1,0:T(8,128)(2,1)} fusion(f32[4,512,2048]{2,1,0:T(8,128)} %get-tuple-element.489, f32[4,512,2048]{2,1,0:T(8,128)S(1)} %fusion.154, f32[4,512]{1,0:T(4,128)} %get-tuple-element.490, f32[4,512]{1,0:T(4,128)S(1)} %dynamic-slice_bitcast_fusion.2, pred[512,2048]{1,0:T(8,128)(4,1)} %copy-done.1), kind=kLoop, calls=%fused_computation.19.clone.1 | loop fusion | flops 25165824 | bytes 43008000 | tf_op jit(solution)/shard_map/while/body/eval_jaxpr/while/body/eval_jaxpr/convert_element_type | solution.py:250
  732.4 11.1 %dynamic_update_slice.73 = f32[4,512,4,64]{1,0,3,2:T(4,128)} dynamic-update-slice(f32[4,512,4,64]{1,0,3,2:T(4,128)} %get-tuple-element.534, f32[1,512,4,64]{1,0,3,2:T(1,128)S(1)} %copy.107, s32[]{:T(128)S(6)} %copy.133, s32[]{:T(128)} %constant.205.clone.1..sunk, s32[]{:T(128)} %constant.205.clone.1..sunk, s32[]{:T(128)} %constant.205.clone.1..sunk) | dynamic-update-slice | bytes 1048580 | tf_op jit(solution)/shard_map/while/body/eval_jaxpr/while/body/jit(dynamic_update_index_in_dim)/dynamic_update_slice | solution.py:274
  756.1 11.6 %multiply_reduce_fusion.4 = (f32[4,512]{1,0:T(4,128)}, f32[4,512,2048]{2,1,0:T(8,128)}) fusion(f32[4,512,2048]{2,1,0:T(8,128)S(1)} %fusion.154, f32[4,512]{1,0:T(4,128)S(1)} %dynamic-slice_bitcast_fusion.2, pred[512,2048]{1,0:T(8,128)(4,1)} %copy-done.1, bf16[2048,4,64]{0,2,1:T(8,128)(2,1)} %get-tuple-element.554, ...), kind=kOutput, calls=%fused_computation.20.clone.1 | convolution fusion | flops 557840384 | bytes 35930116 | tf_op jit(solution)/shard_map/while/body/eval_jaxpr/while/body/eval_jaxpr/qhd,khd->hqk/dot_general | solution.py:246
  767.7 11.0 %multiply_convert_fusion.4 = bf16[4,512,2048]{2,1,0:T(8,128)(2,1)} fusion(f32[4,512,2048]{2,1,0:T(8,128)} %get-tuple-element.489, f32[4,512,2048]{2,1,0:T(8,128)S(1)} %fusion.154, f32[4,512]{1,0:T(4,128)} %get-tuple-element.490, f32[4,512]{1,0:T(4,128)S(1)} %dynamic-slice_bitcast_fusion.2, pred[512,2048]{1,0:T(8,128)(4,1)} %copy-done.1), kind=kLoop, calls=%fused_computation.19.clone.1 | loop fusion | flops 25165824 | bytes 43008000 | tf_op jit(solution)/shard_map/while/body/eval_jaxpr/while/body/eval_jaxpr/convert_element_type | solution.py:250
  790.2 11.1 %dynamic_update_slice.73 = f32[4,512,4,64]{1,0,3,2:T(4,128)} dynamic-update-slice(f32[4,512,4,64]{1,0,3,2:T(4,128)} %get-tuple-element.534, f32[1,512,4,64]{1,0,3,2:T(1,128)S(1)} %copy.107, s32[]{:T(128)S(6)} %copy.133, s32[]{:T(128)} %constant.205.clone.1..sunk, s32[]{:T(128)} %constant.205.clone.1..sunk, s32[]{:T(128)} %constant.205.clone.1..sunk) | dynamic-update-slice | bytes 1048580 | tf_op jit(solution)/shard_map/while/body/eval_jaxpr/while/body/jit(dynamic_update_index_in_dim)/dynamic_update_slice | solution.py:274
  834.4 37.3 %reduce-scatter.18.cloned.1.call-done = bf16[32,1024]{1,0:T(8,128)(2,1)} async-done(((bf16[256,1024]{1,0:T(8,128)(2,1)}), bf16[32,1024]{1,0:T(8,128)(2,1)}) %reduce-scatter.18.cloned.1.call-update) | async-done | bytes 65552 | tf_op jit(solution)/shard_map/reduce_scatter | solution.py:306
  873.2 67.0 %reduce-scatter.16.cloned.1.call-done = bf16[128,3,256]{2,0,1:T(8,128)(2,1)} async-done(((bf16[1024,3,256]{2,0,1:T(8,128)(2,1)}), bf16[128,3,256]{2,0,1:T(8,128)(2,1)}) %reduce-scatter.16.cloned.1.call-update) | async-done | bytes 196624 | tf_op jit(solution)/shard_map/reduce_scatter | solution.py:300
  944.4 41.8 %reduce-scatter.14.cloned.1.call-done = bf16[512,1024]{1,0:T(8,128)(2,1)} async-done(((bf16[2048,1024]{1,0:T(8,128)(2,1)}), bf16[512,1024]{1,0:T(8,128)(2,1)}) %reduce-scatter.14.cloned.1.call-update) | async-done | bytes 1048592 | tf_op jit(solution)/shard_map/reduce_scatter | solution.py:291
  990.4 39.7 %all-reduce.7 = (f32[]{:T(128)}, f32[2,1024]{1,0:T(2,128)S(1)}) all-reduce(f32[]{:T(128)S(6)} %add.287, f32[2,1024]{1,0:T(2,128)S(1)} %pad_maximum_fusion.1), channel_id=1, replica_groups=mesh['dp'=8,'tensor'=4] {'dp','tensor'}, use_global_device_ids=true, to_apply=%region_30.31 | all-reduce | flops 2049 | bytes 16392 | tf_op jit(solution)/shard_map/psum | solution.py:326
  (334 shorter events, 337.8 us)
Async XLA Ops:
  7.2 54.4 %all-gather.9.cloned.1.call-start = ((), (), s32[]{:S(2)}) async-start(), calls=%async_computation.8 | async-start | bytes 1769472 | tf_op jit(solution)/shard_map/all_gather | solution.py:147
  9.1 88.4 %all-gather.7.cloned.1.call-start = ((), (), s32[]{:S(2)}) async-start(), calls=%async_computation.7 | async-start | bytes 5242880 | tf_op jit(solution)/shard_map/all_gather | solution.py:160
  16.3 231.6 %reduce-scatter.8.cloned.1.call-start = ((), (), s32[]{:S(2)}) async-start(), calls=%async_computation.9 | async-start | bytes 10485760 | tf_op jit(solution)/shard_map/reduce_scatter | solution.py:201
  176.0 196.1 %all-gather.11.cloned.1.call-start = ((), (), s32[]{:S(2)}) async-start(), calls=%async_computation.10 | async-start | bytes 5242880 | tf_op jit(solution)/shard_map/all_gather | solution.py:208
  251.7 135.9 %all-gather.13.cloned.1.call-start = ((), (), s32[]{:S(2)}) async-start(), calls=%async_computation.11 | async-start | bytes 2359296 | tf_op jit(solution)/shard_map/all_gather | solution.py:150
  253.6 142.3 %all-gather.15.cloned.1.call-start = ((), (), s32[]{:S(2)}) async-start(), calls=%async_computation.13 | async-start | bytes 5242880 | tf_op jit(solution)/shard_map/all_gather | solution.py:219
  254.2 218.8 %reduce-scatter.12.cloned.1.call-start = ((), (), s32[]{:S(2)}) async-start(), calls=%async_computation.14 | async-start | bytes 5242880 | tf_op jit(solution)/shard_map/reduce_scatter | solution.py:224
  259.7 23.9 %collective-permute-start = (bf16[128,2,1024]{2,1,0:T(2,128)(2,1)S(1)}, bf16[128,2,1024]{2,1,0:T(2,128)(2,1)S(1)}, u32[]{:S(2)}, u32[]{:S(2)}) collective-permute-start(bf16[128,2,1024]{2,1,0:T(2,128)(2,1)S(1)} %get-tuple-element.332), channel_id=1, source_target_pairs={{0,4},{4,8},{8,12},{12,16},{16,20},{20,24},{24,28},{28,0},{1,5},{5... | collective-permute-start | bytes 1572872 | tf_op jit(solution)/shard_map/ppermute | solution.py:40
  261.2 24.9 %collective-permute-start.1 = (bf16[128,2,1024]{2,1,0:T(2,128)(2,1)S(1)}, bf16[128,2,1024]{2,1,0:T(2,128)(2,1)}, u32[]{:S(2)}, u32[]{:S(2)}) collective-permute-start(bf16[128,2,1024]{2,1,0:T(2,128)(2,1)S(1)} %get-tuple-element.332), channel_id=1, source_target_pairs={{0,28},{4,0},{8,4},{12,8},{16,12},{20,16},{24,20},{28,24},{1,29},{... | collective-permute-start | bytes 1572872 | tf_op jit(solution)/shard_map/ppermute | solution.py:45
  283.6 26.9 %collective-permute-start.2 = (bf16[128,2,1024]{2,1,0:T(2,128)(2,1)S(1)}, bf16[128,2,1024]{2,1,0:T(2,128)(2,1)}, u32[]{:S(2)}, u32[]{:S(2)}) collective-permute-start(bf16[128,2,1024]{2,1,0:T(2,128)(2,1)S(1)} %collective-permute-done), channel_id=1, source_target_pairs={{0,4},{4,8},{8,12},{12,16},{16,20},{20,24},{24,28},{28,0},{1,5},{5... | collective-permute-start | bytes 1572872 | tf_op jit(solution)/shard_map/ppermute | solution.py:40
  286.1 27.0 %collective-permute-start.3 = (bf16[128,2,1024]{2,1,0:T(2,128)(2,1)}, bf16[128,2,1024]{2,1,0:T(2,128)(2,1)}, u32[]{:S(2)}, u32[]{:S(2)}) collective-permute-start(bf16[128,2,1024]{2,1,0:T(2,128)(2,1)} %collective-permute-done.1), channel_id=1, source_target_pairs={{0,28},{4,0},{8,4},{12,8},{16,12},{20,16},{24,20},{28,24},{1,29},{... | collective-permute-start | bytes 1572872 | tf_op jit(solution)/shard_map/ppermute | solution.py:45
  310.5 35.4 %collective-permute-start.4 = (bf16[128,2,1024]{2,1,0:T(2,128)(2,1)}, bf16[128,2,1024]{2,1,0:T(2,128)(2,1)}, u32[]{:S(2)}, u32[]{:S(2)}) collective-permute-start(bf16[128,2,1024]{2,1,0:T(2,128)(2,1)} %collective-permute-done.2), channel_id=1, source_target_pairs={{0,4},{4,8},{8,12},{12,16},{16,20},{20,24},{24,28},{28,0},{1,5},{5... | collective-permute-start | bytes 1572872 | tf_op jit(solution)/shard_map/ppermute | solution.py:40
  313.1 44.1 %collective-permute-start.5 = (bf16[128,2,1024]{2,1,0:T(2,128)(2,1)}, bf16[128,2,1024]{2,1,0:T(2,128)(2,1)S(1)}, u32[]{:S(2)}, u32[]{:S(2)}) collective-permute-start(bf16[128,2,1024]{2,1,0:T(2,128)(2,1)} %collective-permute-done.3), channel_id=1, source_target_pairs={{0,28},{4,0},{8,4},{12,8},{16,12},{20,16},{24,20},{28,24},{1,29},{... | collective-permute-start | bytes 1572872 | tf_op jit(solution)/shard_map/ppermute | solution.py:45
  345.9 19.1 %collective-permute-start.6 = (bf16[128,2,1024]{2,1,0:T(2,128)(2,1)}, bf16[128,2,1024]{2,1,0:T(2,128)(2,1)S(1)}, u32[]{:S(2)}, u32[]{:S(2)}) collective-permute-start(bf16[128,2,1024]{2,1,0:T(2,128)(2,1)} %collective-permute-done.4), channel_id=1, source_target_pairs={{0,4},{4,8},{8,12},{12,16},{16,20},{20,24},{24,28},{28,0},{1,5},{5... | collective-permute-start | bytes 1572872 | tf_op jit(solution)/shard_map/ppermute | solution.py:40
  428.2 91.7 %reduce-scatter.10.cloned.1.call-start = ((), (), s32[]{:S(2)}) async-start(), calls=%async_computation.12 | async-start | bytes 5242880 | tf_op jit(solution)/shard_map/reduce_scatter | solution.py:211
  438.1 122.6 %all-gather.17.cloned.1.call-start = ((), (), s32[]{:S(2)}) async-start(), calls=%async_computation.15 | async-start | bytes 5242880 | tf_op jit(solution)/shard_map/all_gather | solution.py:232
  526.0 303.9 %all-reduce.10.cloned.1.call-start = ((), (), s32[]{:S(2)}) async-start(), calls=%async_computation.20 | async-start | bytes 8388608
  551.0 281.7 %reduce-scatter.20.cloned.1.call-start = ((), (), s32[]{:S(2)}) async-start(), calls=%async_computation.19 | async-start | bytes 2359296 | tf_op jit(solution)/shard_map/reduce_scatter | solution.py:315
  560.6 311.1 %reduce-scatter.18.cloned.1.call-start = ((), (), s32[]{:S(2)}) async-start(), calls=%async_computation.18 | async-start | bytes 589824 | tf_op jit(solution)/shard_map/reduce_scatter | solution.py:306
  809.6 130.6 %reduce-scatter.16.cloned.1.call-start = ((), (), s32[]{:S(2)}) async-start(), calls=%async_computation.17 | async-start | bytes 1769472 | tf_op jit(solution)/shard_map/reduce_scatter | solution.py:300
  820.9 165.3 %reduce-scatter.14.cloned.1.call-start = ((), (), s32[]{:S(2)}) async-start(), calls=%async_computation.16 | async-start | bytes 5242880 | tf_op jit(solution)/shard_map/reduce_scatter | solution.py:291
  828.0 158.2 %copy-start.3 = (bf16[512,1024]{1,0:T(8,128)(2,1)S(1)}, bf16[512,1024]{1,0:T(8,128)(2,1)}, u32[]{:S(2)}) copy-start(bf16[512,1024]{1,0:T(8,128)(2,1)} %param.22) | copy-start | bytes 3145732
  828.0 158.2 %copy-start.38 = (f32[1,1024]{1,0:T(1,128)S(1)}, f32[1,1024]{1,0:T(1,128)}, u32[]{:S(2)}) copy-start(f32[1,1024]{1,0:T(1,128)} %copy-done.37) | copy-start | bytes 12292
  828.0 158.2 %copy-start.42 = (f32[512]{0:T(512)S(1)}, f32[512]{0:T(512)}, u32[]{:S(2)}) copy-start(f32[512]{0:T(512)} %copy-done.41) | copy-start | bytes 6148
  828.0 159.9 %copy-start.49 = (f32[512]{0:T(512)S(1)}, f32[512]{0:T(512)}, u32[]{:S(2)}) copy-start(f32[512]{0:T(512)} %copy-done.48) | copy-start | bytes 6148
  828.1 159.9 %copy-start.45 = (f32[512]{0:T(512)S(1)}, f32[512]{0:T(512)}, u32[]{:S(2)}) copy-start(f32[512]{0:T(512)} %copy-done.44) | copy-start | bytes 6148
  828.1 162.3 %copy-start.50 = (f32[1024]{0:T(1024)S(1)}, f32[1024]{0:T(1024)}, u32[]{:S(2)}) copy-start(f32[1024]{0:T(1024)} %get-tuple-element.261) | copy-start | bytes 12292
  828.1 204.1 %copy-start.43 = (f32[2,1024]{1,0:T(2,128)S(1)}, f32[2,1024]{1,0:T(2,128)}, u32[]{:S(2)}) copy-start(f32[2,1024]{1,0:T(2,128)} %param.37) | copy-start | bytes 24580
  828.1 204.1 %copy-start.51 = (f32[2,1024]{1,0:T(2,128)S(1)}, f32[2,1024]{1,0:T(2,128)}, u32[]{:S(2)}) copy-start(f32[2,1024]{1,0:T(2,128)} %param.38) | copy-start | bytes 24580
  828.1 204.1 %copy-start.52 = (f32[2,1024]{1,0:T(2,128)S(1)}, f32[2,1024]{1,0:T(2,128)}, u32[]{:S(2)}) copy-start(f32[2,1024]{1,0:T(2,128)} %param.39) | copy-start | bytes 24580
  828.1 204.8 %copy-start.7 = (f32[512,1024]{1,0:T(8,128)S(1)}, f32[512,1024]{1,0:T(8,128)}, u32[]{:S(2)}) copy-start(f32[512,1024]{1,0:T(8,128)} %copy-done.6) | copy-start | bytes 6291460
  828.1 204.8 %copy-start.47 = (f32[512]{0:T(512)S(1)}, f32[512]{0:T(512)}, u32[]{:S(2)}) copy-start(f32[512]{0:T(512)} %copy-done.46) | copy-start | bytes 6148
  (64 other events, 500.1 us)
Sparse Core Ops, SparseCore 0:
  10.7 50.9 all-gather.8
  63.8 33.7 all-gather.6
  176.1 71.7 reduce-scatter.7
  251.8 34.4 all-gather.10
  289.1 71.5 all-gather.12
  362.2 33.6 all-gather.14
  428.4 44.5 reduce-scatter.11
  475.4 44.4 reduce-scatter.9
  526.2 34.4 all-gather.16
  564.7 156.3 all-reduce.9
  725.0 66.6 reduce-scatter.19
  809.7 61.9 reduce-scatter.17
  875.7 64.4 reduce-scatter.15
  942.7 43.4 reduce-scatter.13
